TPU v7x, 256 devices: a whole 4x4x8 slice. The times are simulated.
256 devices in a mesh: wa: 64 (over z, x, core), gy: 4 (over y).
Axes of the slice: x: 4, y: 4, z: 8, core: 2. Of those that a mesh axis runs over, the one named last changes fastest.
Arguments:
- bricks: bfloat16 [1024, 64, 4096], P('wa', None, 'gy'), may hold values from -6 to 6
- brick_coords: int32 [1024, 2], P('wa'), may hold values from 0 to 15, as said below
- counts: int32 [64], P('wa'), may hold values from 1 to 16, as said below
- green_kernel: bfloat16 [64, 2048, 2048], P('wa', 'gy'), may hold values from 0.19921875 to 4
Outputs:
- potential_hat: bfloat16 [64, 2, 2048, 2048], P('wa', None, 'gy')
Inputs may be any that keep to these rules, and one draw needn't show every extreme that they name: Each owner's occupied slots are its first counts[o] slots; in every draw one owner fills all 16. `brick_coords`: column entries are below 2, z bricks below 16; the pairs of one owner's 16 slots are distinct.
All inputs are finite; a program needn't handle non-finite values.
Results may differ from a plain program's by a relative error of at most 0.0072.
Values may be sent and summed in bfloat16 or wider, within the bound.
A program may use at most 128 MiB of HBM per device.

v0:
```python
import math
import jax
import jax.numpy as jnp
import ml_dtypes
import numpy as np
from jax import lax
from jax.sharding import PartitionSpec as P

BX = 16
BZ = 16
COL_DEV = 2


def wave(positions, frequency, length, factor):
    angles = positions[:, None] * frequency[None, :] % length * (2.0 * math.pi / length)
    return (
        (np.cos(angles) * factor).astype(ml_dtypes.bfloat16),
        (np.sin(angles) * factor).astype(ml_dtypes.bfloat16),
    )


def on_device(bricks, brick_coords, counts, green_kernel):
    depth_count, kx_count, length = green_kernel.shape
    owners = lax.axis_size("wa")
    groups = lax.axis_size("gy")
    depth_total = depth_count * owners
    slot_count, edge, cells = bricks.shape
    rows_brick = cells // edge
    depth_cosine, depth_sine = wave(
        np.arange(BZ * edge), np.arange(depth_total), length, 1.0 / math.sqrt(BZ * edge)
    )
    table = np.concatenate(
        [depth_cosine, (-depth_sine.astype(np.float32)).astype(ml_dtypes.bfloat16)], 1
    )
    table = jnp.asarray(table.reshape(BZ, edge, 2 * depth_total).transpose(0, 2, 1))
    picked = jnp.take(table, brick_coords[:, 1], axis=0)
    alive = jnp.arange(slot_count, dtype=jnp.int32) < counts[0]
    mine = (brick_coords[:, 0][None, :] == jnp.arange(COL_DEV, dtype=jnp.int32)[:, None]) & alive[
        None, :
    ]
    mixing = picked[None] * mine[:, :, None, None].astype(jnp.bfloat16)
    sums = jnp.einsum("gsqz,szc->gqc", mixing, bricks, preferred_element_type=jnp.float32)
    spectra = sums.astype(jnp.bfloat16).reshape(COL_DEV, 2, depth_total, rows_brick, edge)
    spectra = spectra.transpose(2, 1, 3, 0, 4).reshape(depth_total, 2, rows_brick, COL_DEV * edge)
    arrived = lax.all_to_all(spectra, "wa", split_axis=0, concat_axis=0, tiled=True)
    wide = BX // COL_DEV
    brick_rows = owners // wide
    local_rows = brick_rows * rows_brick
    layout = arrived.reshape(brick_rows, wide, 2, rows_brick, COL_DEV * edge)
    layout = layout.transpose(2, 0, 3, 1, 4).reshape(2, local_rows, BX * edge)
    cosine, sine = wave(np.arange(BX * edge), np.arange(length), length, 1.0 / math.sqrt(BX * edge))
    negative = (-sine.astype(np.float32)).astype(ml_dtypes.bfloat16)
    both = jnp.asarray(np.stack([np.stack([cosine, sine]), np.stack([negative, cosine])], 0))
    planes = jnp.einsum("pyx,opxq->oyq", layout, both, preferred_element_type=jnp.float32).astype(
        jnp.bfloat16
    )
    regrouped = lax.all_to_all(planes, "gy", split_axis=2, concat_axis=1, tiled=True)
    every = np.arange(groups * local_rows)
    source, within = (every // local_rows, every % local_rows)
    global_rows = within // rows_brick * edge + source * rows_brick + within % rows_brick
    cosine, sine = wave(global_rows, np.arange(length), length, 1.0 / math.sqrt(brick_rows * edge))
    negative = (-sine.astype(np.float32)).astype(ml_dtypes.bfloat16)
    both = jnp.asarray(np.stack([np.stack([cosine, sine]), np.stack([negative, cosine])], 0))
    final = jnp.einsum("pyx,opyr->oxr", regrouped, both, preferred_element_type=jnp.float32)
    return (final * green_kernel.astype(jnp.float32)).astype(jnp.bfloat16)[None]


def solution(mesh):
    return jax.shard_map(
        on_device,
        mesh=mesh,
        in_specs=(P("wa", None, "gy"), P("wa", None), P("wa"), P("wa", "gy", None)),
        out_specs=P("wa", None, "gy", None),
        check_vma=False,
    )
```

profile of v0, /device:TPU:1, one launch (start us, length us, event | category | flops | bytes accessed | tf_op | source)
XLA Modules:
  0.0 86.4 jit_solution(8450380916489983388)
XLA Ops:
  0.0 0.0 copy-start
  0.0 0.8 and_bitcast_fusion
  0.8 0.8 fusion.15
  2.3 1.5 %gather_fusion = bf16[16,128,64]{1,2,0:T(8,128)(2,1)S(1)} fusion(bf16[16,128,64]{1,2,0:T(8,128)(2,1)} %constant.22.clone, s32[1024]{0:T(1024)S(1)} %pad_clamp_fusion), kind=kCustom, calls=%fused_computation | custom fusion | bytes 524352 | tf_op jit(solution)/shard_map/jit(_take)/gather | solution.py:36
  3.8 0.1 broadcast_select_fusion
  3.9 0.0 copy-done
  4.0 1.6 %fusion.9 = bf16[2,128,1024]{2,1,0:T(8,128)(2,1)} fusion(bf16[16,64,1024]{2,1,0:T(8,128)(2,1)S(1)} %copy-done, bf16[2,16]{1,0:T(2,128)(2,1)S(1)} %and_convert_fusion, bf16[16,128,64]{1,2,0:T(8,128)(2,1)S(1)} %broadcast_select_fusion), kind=kOutput, calls=%fused_computation.11 | convolution fusion | flops 537395200 | bytes 2883648 | tf_op jit(solution)/shard_map/gsqz,szc->gqc/dot_general | solution.py:42
  5.6 1.8 %reshape.58 = bf16[2,2,64,16,64]{4,3,2,1,0:T(8,128)(2,1)S(1)} reshape(bf16[2,128,1024]{2,1,0:T(8,128)(2,1)} %fusion.9) | data formatting | bytes 1048576 | tf_op jit(solution)/shard_map/reshape | solution.py:43
  7.3 2.6 %copy.22 = bf16[2,2,64,16,64]{4,0,3,1,2:T(2,128)(2,1)} copy(bf16[2,2,64,16,64]{4,3,2,1,0:T(8,128)(2,1)S(1)} %reshape.58) | data formatting | bytes 1048576 | tf_op jit(solution)/shard_map/reshape | solution.py:43
  9.9 2.4 %reshape.59 = bf16[64,2,16,128]{3,2,1,0:T(8,128)(2,1)S(1)} reshape(bf16[64,2,16,2,64]{4,3,2,1,0:T(2,128)(2,1)} %bitcast.62) | data formatting | bytes 1048576 | tf_op jit(solution)/shard_map/reshape | solution.py:44
  12.3 30.5 %all_to_all.23 = bf16[64,2,16,128]{3,2,1,0:T(8,128)(2,1)S(1)} all-to-all(bf16[64,2,16,128]{3,2,1,0:T(8,128)(2,1)S(1)} %reshape.59), channel_id=1, replica_groups=mesh['wa'=64,'gy'=4] {'wa'}, dimensions={0} | all-to-all | bytes 1048576 | tf_op jit(solution)/shard_map/all_to_all | solution.py:45
  42.8 0.2 copy.13
  43.0 1.0 %reshape.73 = bf16[2,128,1024,1]{2,1,0,3:T(8,128)(2,1)} reshape(bf16[2,8,16,8,128]{4,3,2,1,0:T(8,128)(2,1)S(1)} %copy.13) | data formatting | bytes 1048576 | tf_op jit(solution)/shard_map/reshape | solution.py:50
  44.1 8.3 %fusion.3 = bf16[2,128,2048]{2,1,0:T(8,128)(2,1)S(1)} fusion(bf16[2,128,1024,1]{2,1,0,3:T(8,128)(2,1)} %reshape.73, bf16[2,2,1024,2048]{3,2,1,0:T(8,128)(2,1)} %constant.23.clone), kind=kOutput, calls=%fused_computation.6 | convolution fusion | flops 2148007936 | bytes 18350080 | tf_op jit(solution)/shard_map/pyx,opxq->oyq/dot_general | solution.py:54
  52.4 2.0 %copy.14 = bf16[2,128,2048]{1,0,2:T(2,128)(2,1)} copy(bf16[2,128,2048]{2,1,0:T(8,128)(2,1)S(1)} %fusion.3) | data formatting | bytes 2097152 | tf_op jit(solution)/shard_map/convert_element_type | solution.py:54
  54.4 4.2 %all-to-all-start.1 = ((bf16[2,128,2048]{1,0,2:T(2,128)(2,1)}), bf16[2,128,2048]{1,0,2:T(2,128)(2,1)S(1)}, u32[]{:S(2)}, u32[]{:S(2)}) async-start(bf16[2,128,2048]{1,0,2:T(2,128)(2,1)} %copy.14), calls=%async_computation.1 | async-start | bytes 2097152 | tf_op jit(solution)/shard_map/all_to_all | solution.py:57
  58.5 4.1 %bitcast_convert_fusion = f32[512,2048]{1,0:T(8,128)} fusion(bf16[1,512,2048]{2,1,0:T(8,128)(2,1)} %param.10), kind=kLoop, calls=%fused_computation.7 | loop fusion | flops 1048576 | bytes 6291456 | tf_op jit(solution)/shard_map/mul | solution.py:65
  62.6 10.4 %all-to-all-done.1 = bf16[2,128,2048]{1,0,2:T(2,128)(2,1)S(1)} async-done(((bf16[2,128,2048]{1,0,2:T(2,128)(2,1)}), bf16[2,128,2048]{1,0,2:T(2,128)(2,1)S(1)}, u32[]{:S(2)}, u32[]{:S(2)}) %all-to-all-start.1) | async-done | bytes 1048608 | tf_op jit(solution)/shard_map/all_to_all | solution.py:57
  73.0 1.8 %copy.21 = bf16[2,128,4,512]{1,2,3,0:T(4,128)(2,1)} copy(bf16[2,128,4,512]{1,0,3,2:T(2,128)(2,1)S(1)} %bitcast.61) | data formatting | bytes 2097152 | tf_op jit(solution)/shard_map/all_to_all | solution.py:57
  74.8 1.5 %reshape.75 = bf16[2,512,512,1]{1,2,0,3:T(8,128)(2,1)S(1)} reshape(bf16[2,4,128,512]{2,1,3,0:T(4,128)(2,1)} %bitcast.63) | data formatting | bytes 2097152 | tf_op jit(solution)/shard_map/all_to_all | solution.py:57
  76.3 10.1 %fusion.1 = bf16[1,2,512,2048]{3,2,1,0:T(8,128)(2,1)} fusion(f32[512,2048]{1,0:T(8,128)} %bitcast_convert_fusion, bf16[2,512,512,1]{1,2,0,3:T(8,128)(2,1)S(1)} %reshape.75, bf16[2,2,512,2048]{3,2,1,0:T(8,128)(2,1)} %constant.24.clone), kind=kOutput, calls=%fused_computation.3 | convolution fusion | flops 4299161600 | bytes 17825792 | tf_op jit(solution)/shard_map/pyx,opyr->oxr/dot_general | solution.py:64
  (3 shorter events, 0.0 us)
Async XLA Ops:
  0.0 3.9 %copy-start = (bf16[16,64,1024]{2,1,0:T(8,128)(2,1)S(1)}, bf16[16,64,1024]{2,1,0:T(8,128)(2,1)}, u32[]{:S(2)}) copy-start(bf16[16,64,1024]{2,1,0:T(8,128)(2,1)} %param.7) | copy-start | bytes 6291460
  54.4 18.7 %all-to-all-start.1 = ((bf16[2,128,2048]{1,0,2:T(2,128)(2,1)}), bf16[2,128,2048]{1,0,2:T(2,128)(2,1)S(1)}, u32[]{:S(2)}, u32[]{:S(2)}) async-start(bf16[2,128,2048]{1,0,2:T(2,128)(2,1)} %copy.14), calls=%async_computation.1 | async-start | bytes 2097152 | tf_op jit(solution)/shard_map/all_to_all | solution.py:57
where the time goes:
time: 86.7 us; the launch traced here: 86.4 us
  blocking collectives  30.5 us (35%)
  matrix products  20 us (23%)
  local copies, waits for them, and re-layouts  14.8 us (17%)
  waiting for transfers between devices  10.4 us (12%)
  other arithmetic  5.76 us (7%)
  starting transfers between devices  4.18 us (5%)
    all_to_all x1, blocking collectives, on_device(): lax.all_to_all(spectra, 'wa', split_axis=0, concat_axis=0, tiled=True)  30.5 us
    all_to_all x1, waiting for transfers between devices, on_device(): lax.all_to_all(planes, 'gy', split_axis=2, concat_axis=1, tiled=True)  10.4 us
    dot_general x1, matrix products, on_device(): jnp.einsum('pyx,opyr->oxr', regrouped, both, preferred_element_type=jnp.f...  10.1 us
    dot_general x1, matrix products, on_device(): jnp.einsum('pyx,opxq->oyq', layout, both, preferred_element_type=jnp.floa...  8.29 us
    reshape x2, local copies, waits for them, and re-layouts, on_device(): sums.astype(jnp.bfloat16).reshape(COL_DEV, 2, depth_total, rows_brick, edge)  4.34 us
    all_to_all x1, starting transfers between devices, on_device(): lax.all_to_all(planes, 'gy', split_axis=2, concat_axis=1, tiled=True)  4.18 us
    mul x1, other arithmetic, on_device(): return (final * green_kernel.astype(jnp.float32)).astype(jnp.bfloat16)[None]  4.06 us
    all_to_all x2, local copies, waits for them, and re-layouts, on_device(): lax.all_to_all(planes, 'gy', split_axis=2, concat_axis=1, tiled=True)  3.25 us
  transfers between devices with their start and end apart: 1, of which 1 were waited for; matrix products, arithmetic and copies ran while one was open for 5% of the time, Pallas kernels for 0%

commit v1 on v0

--- a/solution.py
+++ b/solution.py
@@ -54,7 +54,10 @@
     planes = jnp.einsum("pyx,opxq->oyq", layout, both, preferred_element_type=jnp.float32).astype(
         jnp.bfloat16
     )
-    regrouped = lax.all_to_all(planes, "gy", split_axis=2, concat_axis=1, tiled=True)
+    regrouped = jnp.concatenate(
+        lax.all_to_all(jnp.stack(jnp.split(planes, lax.axis_size("gy"), axis=2)), "gy", 0, 0),
+        axis=1,
+    )
     every = np.arange(groups * local_rows)
     source, within = (every // local_rows, every % local_rows)
     global_rows = within // rows_brick * edge + source * rows_brick + within % rows_brick

time: 86.7 us -> 82 us (0.946)
  local copies, waits for them, and re-layouts: 14.8 us -> 8.9 us
  other arithmetic: 5.76 us -> 6.86 us
    all_to_all x2 -> x0, local copies, waits for them, and re-layouts: 3.25 us -> none  [on_device(): lax.all_to_all(planes, 'gy', split_axis=2, concat_axis=1, tiled=True)]
    convert_element_type x1 -> x0, local copies, waits for them, and re-layouts: 2 us -> none  [on_device(): jnp.einsum('pyx,opxq->oyq', layout, both, preferred_element_type=jnp.floa...]
    another operation x0 -> x1, other arithmetic: none -> 1.1 us  [on_device(): jnp.stack(jnp.split(planes, lax.axis_size('gy'), axis=2))]
where the time goes in v1:
time: 82 us; the launch traced here: 81.6 us
  blocking collectives  30.5 us (37%)
  matrix products  20 us (24%)
  waiting for transfers between devices  10.5 us (13%)
  local copies, waits for them, and re-layouts  8.9 us (11%)
  other arithmetic  6.86 us (8%)
  starting transfers between devices  4.18 us (5%)
    all_to_all x1, blocking collectives, on_device(): lax.all_to_all(spectra, 'wa', split_axis=0, concat_axis=0, tiled=True)  30.5 us
    all_to_all x1, waiting for transfers between devices, on_device(): lax.all_to_all(jnp.stack(jnp.split(planes, lax.axis_size('gy'), axis=2)),...  10.5 us
    dot_general x1, matrix products, on_device(): jnp.einsum('pyx,opyr->oxr', regrouped, both, preferred_element_type=jnp.f...  10.2 us
    dot_general x1, matrix products, on_device(): jnp.einsum('pyx,opxq->oyq', layout, both, preferred_element_type=jnp.floa...  8.12 us
    reshape x2, local copies, waits for them, and re-layouts, on_device(): sums.astype(jnp.bfloat16).reshape(COL_DEV, 2, depth_total, rows_brick, edge)  4.34 us
    all_to_all x1, starting transfers between devices, on_device(): lax.all_to_all(jnp.stack(jnp.split(planes, lax.axis_size('gy'), axis=2)),...  4.18 us
    mul x1, other arithmetic, on_device(): return (final * green_kernel.astype(jnp.float32)).astype(jnp.bfloat16)[None]  4.05 us
    reshape x1, local copies, waits for them, and re-layouts, on_device(): spectra.transpose(2, 1, 3, 0, 4)  2.41 us
  transfers between devices with their start and end apart: 1, of which 1 were waited for; matrix products, arithmetic and copies ran while one was open for 5% of the time, Pallas kernels for 0%

profile of v1, /device:TPU:1, one launch (start us, length us, event | category | flops | bytes accessed | tf_op | source)
XLA Modules:
  0.0 81.6 jit_solution(11149261689291990993)
XLA Ops:
  0.0 0.0 copy-start
  0.0 0.8 %and_bitcast_fusion = pred[16]{0:T(512)(128)(4,1)S(1)} fusion(s32[16,2]{0,1:T(2,128)} %param.8), kind=kLoop, calls=%fused_computation.25 | loop fusion | flops 96 | bytes 80 | tf_op jit(solution)/shard_map/jit(_take)/reduce_and | solution.py:36
  0.8 0.8 fusion.15
  2.3 1.5 %gather_fusion = bf16[16,128,64]{1,2,0:T(8,128)(2,1)S(1)} fusion(bf16[16,128,64]{1,2,0:T(8,128)(2,1)} %constant.22.clone, s32[1024]{0:T(1024)S(1)} %pad_clamp_fusion), kind=kCustom, calls=%fused_computation | custom fusion | bytes 524352 | tf_op jit(solution)/shard_map/jit(_take)/gather | solution.py:36
  3.8 0.1 broadcast_select_fusion
  3.9 0.0 copy-done
  4.0 1.6 %fusion.9 = bf16[2,128,1024]{2,1,0:T(8,128)(2,1)} fusion(bf16[16,64,1024]{2,1,0:T(8,128)(2,1)S(1)} %copy-done, bf16[2,16]{1,0:T(2,128)(2,1)S(1)} %and_convert_fusion, bf16[16,128,64]{1,2,0:T(8,128)(2,1)S(1)} %broadcast_select_fusion), kind=kOutput, calls=%fused_computation.11 | convolution fusion | flops 537395200 | bytes 2883648 | tf_op jit(solution)/shard_map/gsqz,szc->gqc/dot_general | solution.py:42
  5.6 1.8 %reshape.64 = bf16[2,2,64,16,64]{4,3,2,1,0:T(8,128)(2,1)S(1)} reshape(bf16[2,128,1024]{2,1,0:T(8,128)(2,1)} %fusion.9) | data formatting | bytes 1048576 | tf_op jit(solution)/shard_map/reshape | solution.py:43
  7.3 2.6 %copy.18 = bf16[2,2,64,16,64]{4,0,3,1,2:T(2,128)(2,1)} copy(bf16[2,2,64,16,64]{4,3,2,1,0:T(8,128)(2,1)S(1)} %reshape.64) | data formatting | bytes 1048576 | tf_op jit(solution)/shard_map/reshape | solution.py:43
  9.9 2.4 %reshape.65 = bf16[64,2,16,128]{3,2,1,0:T(8,128)(2,1)S(1)} reshape(bf16[64,2,16,2,64]{4,3,2,1,0:T(2,128)(2,1)} %bitcast.68) | data formatting | bytes 1048576 | tf_op jit(solution)/shard_map/reshape | solution.py:44
  12.3 30.5 %all_to_all.10 = bf16[64,2,16,128]{3,2,1,0:T(8,128)(2,1)S(1)} all-to-all(bf16[64,2,16,128]{3,2,1,0:T(8,128)(2,1)S(1)} %reshape.65), channel_id=1, replica_groups=mesh['wa'=64,'gy'=4] {'wa'}, dimensions={0} | all-to-all | bytes 1048576 | tf_op jit(solution)/shard_map/all_to_all | solution.py:45
  42.8 0.2 copy.9
  43.0 0.2 reshape.81
  43.3 8.1 %fusion.3 = bf16[2,128,2048]{2,1,0:T(8,128)(2,1)S(1)} fusion(bf16[2,128,1024,1]{2,1,0,3:T(8,128)(2,1)S(1)} %reshape.81, bf16[2,2,1024,2048]{3,2,1,0:T(8,128)(2,1)} %constant.23.clone), kind=kOutput, calls=%fused_computation.6 | convolution fusion | flops 2148007936 | bytes 18350080 | tf_op jit(solution)/shard_map/pyx,opxq->oyq/dot_general | solution.py:54
  51.4 0.1 slice_bitcast_fusion.3
  51.5 1.1 %pad_maximum_fusion = bf16[4,2,128,512]{3,2,1,0:T(8,128)(2,1)} fusion(bf16[1,2,128,512]{3,2,1,0:T(8,128)(2,1)S(1)} %get-tuple-element.6, bf16[1,2,128,512]{3,2,1,0:T(8,128)(2,1)S(1)} %get-tuple-element.7, bf16[1,2,128,512]{3,2,1,0:T(8,128)(2,1)S(1)} %get-tuple-element.8, bf16[1,2,128,512]{3,2,1,0:T(8,128)(2,1)S(1)} %get-tuple-element.5), kind=kLoop, calls=%fused_computation.12 | loop fusion | flops 1572864 | bytes 2097152 | tf_op jit(solution)/shard_map/stack | solution.py:58
  52.6 4.2 %all-to-all-start.1 = ((bf16[4,2,128,512]{3,2,1,0:T(8,128)(2,1)}), bf16[4,2,128,512]{3,2,1,0:T(8,128)(2,1)S(1)}, u32[]{:S(2)}, u32[]{:S(2)}) async-start(bf16[4,2,128,512]{3,2,1,0:T(8,128)(2,1)} %pad_maximum_fusion), calls=%async_computation.1 | async-start | bytes 2097152 | tf_op jit(solution)/shard_map/all_to_all | solution.py:58
  56.8 4.1 %bitcast_convert_fusion = f32[512,2048]{1,0:T(8,128)} fusion(bf16[1,512,2048]{2,1,0:T(8,128)(2,1)} %param.10), kind=kLoop, calls=%fused_computation.7 | loop fusion | flops 1048576 | bytes 6291456 | tf_op jit(solution)/shard_map/mul | solution.py:68
  60.8 10.5 %all-to-all-done.1 = bf16[4,2,128,512]{3,2,1,0:T(8,128)(2,1)S(1)} async-done(((bf16[4,2,128,512]{3,2,1,0:T(8,128)(2,1)}), bf16[4,2,128,512]{3,2,1,0:T(8,128)(2,1)S(1)}, u32[]{:S(2)}, u32[]{:S(2)}) %all-to-all-start.1) | async-done | bytes 1048608 | tf_op jit(solution)/shard_map/all_to_all | solution.py:58
  71.3 0.1 copy.10
  71.4 10.2 %fusion.1 = bf16[1,2,512,2048]{3,2,1,0:T(8,128)(2,1)} fusion(f32[512,2048]{1,0:T(8,128)} %bitcast_convert_fusion, bf16[2,512,512,1]{2,1,0,3:T(8,128)(2,1)S(1)} %bitcast.70, bf16[2,2,512,2048]{3,2,1,0:T(8,128)(2,1)} %constant.24.clone), kind=kOutput, calls=%fused_computation.3 | convolution fusion | flops 4299161600 | bytes 17825792 | tf_op jit(solution)/shard_map/pyx,opyr->oxr/dot_general | solution.py:67
  (3 shorter events, 0.0 us)
Async XLA Ops:
  0.0 3.9 %copy-start = (bf16[16,64,1024]{2,1,0:T(8,128)(2,1)S(1)}, bf16[16,64,1024]{2,1,0:T(8,128)(2,1)}, u32[]{:S(2)}) copy-start(bf16[16,64,1024]{2,1,0:T(8,128)(2,1)} %param.7) | copy-start | bytes 6291460
  52.6 18.7 %all-to-all-start.1 = ((bf16[4,2,128,512]{3,2,1,0:T(8,128)(2,1)}), bf16[4,2,128,512]{3,2,1,0:T(8,128)(2,1)S(1)}, u32[]{:S(2)}, u32[]{:S(2)}) async-start(bf16[4,2,128,512]{3,2,1,0:T(8,128)(2,1)} %pad_maximum_fusion), calls=%async_computation.1 | async-start | bytes 2097152 | tf_op jit(solution)/shard_map/all_to_all | solution.py:58
